TPU v7x, 32 devices: a whole 2x2x4 slice. The times are simulated.
32 devices in a mesh: dp: 2 (over core), mrow: 8 (over z, y), mcol: 2 (over x).
Axes of the slice: x: 2, y: 2, z: 4, core: 2. Of those that a mesh axis runs over, the one named last changes fastest.
Arguments:
- grad_parts: bfloat16 [2, 18432, 8192], P('dp', 'mrow', 'mcol'), may hold values from -24 to 24, as said below
- master: float32 [18432, 8192], P('mrow', ('mcol', 'dp')), may hold values from -6 to 6
- row_factor: float32 [18432], P('mrow'), may hold values from 0.5 to 5
- col_factor: float32 [8192], P(('mcol', 'dp')), may hold values from 0.5 to 5
Outputs:
- new_master: float32 [18432, 8192], P('mrow', ('mcol', 'dp'))
- new_weights: bfloat16 [18432, 8192], P('mrow', 'mcol')
- new_rows: float32 [18432], P('mrow')
- new_cols: float32 [8192], P(('mcol', 'dp'))
- step: float32 [18432, 8192], P('mrow', ('mcol', 'dp'))
- root_mean: float32 [], replicated
Inputs may be any that keep to these rules, and one draw needn't show every extreme that they name: `grad_parts`: each slice along the first dimension is one data-parallel group's partial gradient.
All inputs are finite; a program needn't handle non-finite values.
Results may differ from a plain program's by a relative error of at most 0.009.
Values may be sent and summed in bfloat16 or wider, within the bound.
A program may use at most 192 MiB of HBM per device.

v0:
```python
import jax
import jax.numpy as jnp
from jax import lax
from jax.sharding import PartitionSpec as P

D = 8192
FF = 18432


DECAY_RATE = 1.0 - 10.0 ** (-0.8)
LEARN_RATE = 0.01
CLIP_LIMIT = 1.0
SQUARE_FLOOR = 1e-30


def finish(grad, old_rows, old_cols, sum_rows, sum_cols, sum_whole):
    squares = grad * grad + SQUARE_FLOOR
    row_local = jnp.sum(squares, axis=1)
    col_local = jnp.sum(squares, axis=0)
    new_rows = DECAY_RATE * old_rows + (1.0 - DECAY_RATE) * sum_rows(row_local) / D
    col_total, row_total = sum_cols((col_local, jnp.sum(new_rows)))
    total = row_total / FF
    new_cols = DECAY_RATE * old_cols + (1.0 - DECAY_RATE) * col_total / FF
    second = new_rows[:, None] * new_cols[None, :] / total
    update = grad / jnp.sqrt(second)
    square_total = sum_whole((jnp.sum(update * update),))[0]
    root_mean = jnp.sqrt(square_total / (FF * D))
    step = update / jnp.maximum(1.0, root_mean / CLIP_LIMIT)
    return (new_rows, new_cols, step, root_mean)


def on_device(grad_parts, master, row_factor, col_factor):

    def sum_cols(values):
        return lax.psum(values, "mrow")

    grad = lax.psum_scatter(grad_parts, "dp", scatter_dimension=2, tiled=True).astype(jnp.float32)[
        0
    ]

    def sum_rows(values):
        return lax.psum(values, ("dp", "mcol"))

    def sum_whole(values):
        return lax.psum(values, ("dp", "mrow", "mcol"))

    new_rows, cols_flat, step_flat, root_mean = finish(
        grad, row_factor, col_factor, sum_rows, sum_cols, sum_whole
    )
    new_flat = master - LEARN_RATE * step_flat
    weights = lax.all_gather(new_flat.astype(jnp.bfloat16), "dp", axis=1, tiled=True)
    return (new_flat, weights, new_rows, cols_flat, step_flat, root_mean)


def solution(mesh):
    placed = (P("dp", "mrow", "mcol"), P("mrow", ("mcol", "dp")), P("mrow"), P(("mcol", "dp")))
    return jax.shard_map(
        on_device,
        mesh=mesh,
        in_specs=placed,
        out_specs=(
            P("mrow", ("mcol", "dp")),
            P("mrow", "mcol"),
            P("mrow"),
            P(("mcol", "dp")),
            P("mrow", ("mcol", "dp")),
            P(),
        ),
        check_vma=False,
    )
```

profile of v0, /device:TPU:0, one launch (start us, length us, event | category | flops | bytes accessed | tf_op | source)
XLA Modules:
  0.0 217.6 jit_solution(11666887581644912188)
XLA Ops:
  7.2 0.0 copy-start.2
  7.2 0.0 copy-start.3
  7.2 0.0 reduce-scatter.2.cloned.1.call-start
  7.2 0.7 reduce-scatter.2.cloned.1.call-update
  7.9 0.0 all-gather.2.cloned.1.call-start
  8.0 31.5 %reduce-scatter.2.cloned.1.call-done = bf16[1,2304,2048]{2,1,0:T(8,128)(2,1)} async-done(((bf16[1,2304,4096]{2,1,0:T(8,128)(2,1)}), bf16[1,2304,2048]{2,1,0:T(8,128)(2,1)}) %reduce-scatter.2.cloned.1.call-update) | async-done | bytes 9437200 | tf_op jit(solution)/shard_map/reduce_scatter | solution.py:37
  39.4 7.6 %fusion.1 = (f32[2048]{0:T(1024)S(1)}, f32[2304]{0:T(1024)S(1)}) fusion(bf16[1,2304,2048]{2,1,0:T(8,128)(2,1)} %reduce-scatter.2.cloned.1.call-done), kind=kLoop, calls=%fused_computation.3 | loop fusion | flops 23588608 | bytes 9454592 | tf_op jit(solution)/shard_map/reduce_sum | solution.py:19
  47.1 12.4 %psum.28 = f32[2304]{0:T(1024)S(1)} all-reduce(f32[2304]{0:T(1024)S(1)} %get-tuple-element.7), channel_id=1, replica_groups=mesh['dp'=2,'mrow'=8,'mcol'=2] {'dp','mcol'}, use_global_device_ids=true, to_apply=%region_2.0 | all-reduce | flops 2304 | bytes 18432 | tf_op jit(solution)/shard_map/psum | solution.py:42
  59.4 0.0 copy-done.2
  59.4 0.6 fusion.4
  60.0 0.0 copy-start
  60.1 22.5 %all-reduce = (f32[]{:T(128)}, f32[2048]{0:T(1024)S(1)}) all-reduce(f32[]{:T(128)} %get-tuple-element.13, f32[2048]{0:T(1024)S(1)} %get-tuple-element.6), channel_id=1, replica_groups=mesh['dp'=2,'mrow'=8,'mcol'=2] {'mrow'}, use_global_device_ids=true, to_apply=%region_6.0 | all-reduce | flops 2049 | bytes 16392 | tf_op jit(solution)/shard_map/psum | solution.py:35
  83.2 0.0 copy-done.3
  83.2 0.0 copy-start.1
  83.2 8.7 %multiply_reduce_fusion = f32[]{:T(128)} fusion(f32[]{:T(128)S(6)} %div.38, f32[2048]{0:T(1024)S(1)} %multiply_add_fusion.1, f32[2304]{0:T(1024)S(1)} %get-tuple-element.23, bf16[1,2304,2048]{2,1,0:T(8,128)(2,1)} %reduce-scatter.2.cloned.1.call-done), kind=kLoop, calls=%fused_computation.6 | loop fusion | flops 28311552 | bytes 9454600 | tf_op jit(solution)/shard_map/reduce_sum | solution.py:26
  92.0 37.1 %psum.31 = f32[]{:T(128)} all-reduce(f32[]{:T(128)} %multiply_reduce_fusion), channel_id=1, replica_groups=mesh['dp'=2,'mrow'=8,'mcol'=2] {'dp','mrow','mcol'}, use_global_device_ids=true, to_apply=%region_8.0 | all-reduce | flops 1 | bytes 8 | tf_op jit(solution)/shard_map/psum | solution.py:45
  129.8 27.5 %fusion.3 = (bf16[2304,2048]{1,0:T(8,128)(2,1)}, f32[2304,2048]{1,0:T(8,128)}, f32[2304,2048]{1,0:T(8,128)}) fusion(f32[2304,2048]{1,0:T(8,128)} %param.5, f32[]{:T(128)S(6)} %max.3, f32[]{:T(128)S(6)} %div.38, f32[2048]{0:T(1024)S(1)} %multiply_add_fusion.1, f32[2304]{0:T(1024)S(1)} %get-tuple-element.23, ...), kind=kLoop, calls=%fused_computation.10 | loop fusion | flops 37748736 | bytes 75514888 | tf_op jit(solution)/shard_map/convert_element_type | solution.py:51
  157.3 0.0 copy-done
  157.3 0.0 copy-done.1
  157.3 0.0 all-gather.2.cloned.1.call-update
  157.3 35.5 %all-gather.2.cloned.1.call-done = bf16[2304,4096]{1,0:T(8,128)(2,1)} async-done(((bf16[2304,2048]{1,0:T(8,128)(2,1)}), bf16[2304,4096]{1,0:T(8,128)(2,1)}) %all-gather.2.cloned.1.call-update) | async-done | bytes 18874384 | tf_op jit(solution)/shard_map/all_gather | solution.py:51
  192.8 16.8 %copy.11 = bf16[2304,4096]{1,0:T(8,128)(2,1)} copy(bf16[2304,4096]{1,0:T(8,128)(2,1)} %all-gather.2.cloned.1.call-done) | data formatting | bytes 37748736
  (1 shorter events, 0.0 us)
Async XLA Ops:
  7.2 52.3 %copy-start.2 = (f32[2304]{0:T(1024)S(1)}, f32[2304]{0:T(1024)}, u32[]{:S(2)}) copy-start(f32[2304]{0:T(1024)} %param.6) | copy-start | bytes 27652
  7.2 76.0 %copy-start.3 = (f32[2048]{0:T(1024)S(1)}, f32[2048]{0:T(1024)}, u32[]{:S(2)}) copy-start(f32[2048]{0:T(1024)} %param.7) | copy-start | bytes 24580
  7.2 32.3 %reduce-scatter.2.cloned.1.call-start = ((), (), s32[]{:S(2)}) async-start(), calls=%async_computation.1 | async-start | bytes 28311552 | tf_op jit(solution)/shard_map/reduce_scatter | solution.py:37
  7.9 184.9 %all-gather.2.cloned.1.call-start = ((), (), s32[]{:S(2)}) async-start(), calls=%async_computation.2 | async-start | bytes 28311552 | tf_op jit(solution)/shard_map/all_gather | solution.py:51
  60.0 97.2 %copy-start = (f32[2304]{0:T(1024)}, f32[2304]{0:T(1024)S(1)}, u32[]{:S(2)}) copy-start(f32[2304]{0:T(1024)S(1)} %get-tuple-element.23) | copy-start | bytes 27652
  83.2 74.1 %copy-start.1 = (f32[2048]{0:T(1024)}, f32[2048]{0:T(1024)S(1)}, u32[]{:S(2)}) copy-start(f32[2048]{0:T(1024)S(1)} %multiply_add_fusion.1) | copy-start | bytes 24580
Sparse Core Ops, SparseCore 0:
  10.3 29.1 reduce-scatter.1
  157.4 35.3 all-gather.1
where the time goes:
time: 218 us
  blocking collectives  71.9 us (33%)
  waiting for transfers between devices  67.7 us (31%)
  other arithmetic  44.5 us (20%)
  local copies, waits for them, and re-layouts  16.8 us (8%)
  between operations  16.6 us (8%)
    psum x1, blocking collectives, sum_whole(): return lax.psum(values, ('dp', 'mrow', 'mcol'))  37.1 us
    all_gather x1, waiting for transfers between devices, on_device(): lax.all_gather(new_flat.astype(jnp.bfloat16), 'dp', axis=1, tiled=True)  35.5 us
    reduce_scatter x1, waiting for transfers between devices, on_device(): lax.psum_scatter(grad_parts, 'dp', scatter_dimension=2, tiled=True)  31.5 us
    convert_element_type x1, other arithmetic, on_device(): new_flat.astype(jnp.bfloat16)  27.5 us
    psum x1, blocking collectives, sum_cols(): return lax.psum(values, 'mrow')  22.5 us
    unnamed x9, local copies, waits for them, and re-layouts  16.8 us
    psum x1, blocking collectives, sum_rows(): return lax.psum(values, ('dp', 'mcol'))  12.4 us
    reduce_sum x1, other arithmetic, finish(): square_total = sum_whole((jnp.sum(update * update),))[0]  8.74 us
  transfers between devices with their start and end apart: 2, of which 2 were waited for; matrix products, arithmetic and copies ran while one was open for 0% of the time, Pallas kernels for 0%

commit v1 on v0

v1 whole, which is shorter than its diff:
```python
import functools

import jax
import jax.numpy as jnp
from jax import lax
from jax.experimental import pallas as pl
from jax.experimental.pallas import tpu as pltpu
from jax.sharding import PartitionSpec as P

DECAY_RATE = 1.0 - 10.0 ** (-0.8)
LEARN_RATE = 0.01
CLIP_LIMIT = 1.0
SQUARE_FLOOR = 1e-30
MESH = pl.DeviceIdType.MESH
LANES = 128
GROUP = 16


def chunk_of(rows, most=256):
    for size in range(min(most, rows), 0, -GROUP):
        if size % GROUP == 0 and rows % size == 0:
            return size
    return rows


def stats_kernel(
    n_dp, n_mrow, n_mcol, chunk,
    grad_ref, master_ref, old_rows_ref, old_cols_ref,
    g_ref, w_recv_ref, new_rows_ref, new_cols_ref, scal_ref,
    gbuf, recv, mbuf, row_col, row_slots, col_slots, sc1_slots, sc2_slots, inv_rows, col_acc,
    own_sem, gsend, grecv, rsend, rrecv, csend, crecv, s1send, s1recv, s2send, s2recv,
    wsend, wrecv, msem, osem,
):
    rows, wc = mbuf.shape
    nc = rows // chunk
    blocks = wc // LANES
    steps = chunk // GROUP
    n_row = n_dp * n_mcol
    width = wc * n_row
    height = rows * n_mrow
    dp, mrow, mcol = lax.axis_index("dp"), lax.axis_index("mrow"), lax.axis_index("mcol")
    q = dp * n_mcol + mcol

    def dp_peer(k):
        return {"dp": lax.rem(dp + k, n_dp), "mrow": mrow, "mcol": mcol}

    def row_peer(k):
        other = lax.rem(q + k, n_row)
        return {"dp": other // n_mcol, "mrow": mrow, "mcol": lax.rem(other, n_mcol)}

    def col_peer(k):
        return {"dp": dp, "mrow": lax.rem(mrow + k, n_mrow), "mcol": mcol}

    def loop(lo, hi, body):
        lax.fori_loop(lo, hi, lambda i, c: (body(i), c)[1], 0)

    def part(i):
        return pl.ds(pl.multiple_of(i * chunk, chunk), chunk)

    def own_copy(i):
        cols = pl.ds(pl.multiple_of(dp * wc, LANES), wc)
        return pltpu.make_async_copy(grad_ref.at[0, part(i), cols], gbuf.at[part(i)], own_sem.at[i])

    def grad_copy(k, i):
        cols = pl.ds(pl.multiple_of(lax.rem(dp + k, n_dp) * wc, LANES), wc)
        return pltpu.make_async_remote_copy(
            src_ref=grad_ref.at[0, part(i), cols], dst_ref=recv.at[k - 1, part(i)],
            send_sem=gsend.at[k - 1, i], recv_sem=grecv.at[k - 1, i],
            device_id=dp_peer(k), device_id_type=MESH)

    def master_copy(i):
        return pltpu.make_async_copy(master_ref.at[part(i)], mbuf.at[part(i)], msem.at[i])

    def out_copy(i):
        return pltpu.make_async_copy(gbuf.at[part(i)], g_ref.at[part(i)], osem.at[i])

    def weight_copy(k, i):
        return pltpu.make_async_remote_copy(
            src_ref=recv.at[0, part(i)], dst_ref=w_recv_ref.at[n_dp - 1 - k, part(i)],
            send_sem=wsend.at[k - 1, i], recv_sem=wrecv.at[k - 1, i],
            device_id=dp_peer(k), device_id_type=MESH)

    def slot_copy(slots, index, peer, send, recv_, k):
        return pltpu.make_async_remote_copy(
            src_ref=slots.at[index], dst_ref=slots.at[index],
            send_sem=send.at[k], recv_sem=recv_.at[k],
            device_id=peer(k), device_id_type=MESH)

    def send_slots(slots, index, peer, send, recv_, n):
        loop(1, n, lambda k: slot_copy(slots, index, peer, send, recv_, k).start())

    def wait_slots(slots, index, peer, send, recv_, n):
        loop(1, n, lambda k: slot_copy(slots, index, peer, send, recv_, k).wait())

    loop(0, nc, lambda i: own_copy(i).start())

    barrier = pltpu.get_barrier_semaphore()
    loop(1, n_row, lambda k: pl.semaphore_signal(barrier, inc=1, device_id=row_peer(k), device_id_type=MESH))
    loop(1, n_mrow, lambda k: pl.semaphore_signal(barrier, inc=1, device_id=col_peer(k), device_id_type=MESH))
    pl.semaphore_wait(barrier, n_row + n_mrow - 2)

    loop(0, nc, lambda i: [grad_copy(k, i).start() for k in range(1, n_dp)])
    loop(0, nc, lambda i: master_copy(i).start())

    col_acc[...] = jnp.zeros_like(col_acc)

    def sum_chunk(i):
        own_copy(i).wait()
        for k in range(1, n_dp):
            grad_copy(k, i).wait_recv()
        base = i * chunk

        def sum_rows(s, carry):
            at = pl.ds(pl.multiple_of(base + s * GROUP, GROUP), GROUP)
            row = None
            for b in range(blocks):
                lanes = slice(b * LANES, (b + 1) * LANES)
                g = gbuf[at, lanes].astype(jnp.float32)
                for k in range(n_dp - 1):
                    g = g + recv[k, at, lanes].astype(jnp.float32)
                gbuf[at, lanes] = g.astype(jnp.bfloat16)
                square = g * g + SQUARE_FLOOR
                row = square if row is None else row + square
                col_acc[:, lanes] += square[:8] + square[8:]
            row_col[pl.ds(pl.multiple_of(base + s * GROUP, GROUP), GROUP), :] = row
            return carry

        lax.fori_loop(0, steps, sum_rows, 0)
        out_copy(i).start()
        row_slots[q, :, part(i)] = jnp.sum(row_col[part(i), :].T, axis=0, keepdims=True)

    loop(0, nc, sum_chunk)
    col_slots[mrow] = jnp.sum(col_acc[...], axis=0, keepdims=True)
    send_slots(col_slots, mrow, col_peer, csend, crecv, n_mrow)
    send_slots(row_slots, q, row_peer, rsend, rrecv, n_row)
    wait_slots(row_slots, q, row_peer, rsend, rrecv, n_row)
    row_sum = row_slots[0]
    for j in range(1, n_row):
        row_sum = row_sum + row_slots[j]
    new_rows = DECAY_RATE * old_rows_ref[...] + (1.0 - DECAY_RATE) * row_sum / width
    new_rows_ref[...] = new_rows
    inv_rows[...] = lax.rsqrt(new_rows)
    row_mass = jnp.sum(new_rows)

    def spread(i):
        row_col[part(i), :] = jnp.broadcast_to(inv_rows[:, part(i)], (LANES, chunk)).T

    loop(0, nc, spread)
    wait_slots(col_slots, mrow, col_peer, csend, crecv, n_mrow)
    col_sum = lax.fori_loop(1, n_mrow, lambda j, acc: acc + col_slots[j], col_slots[0])
    new_cols = DECAY_RATE * old_cols_ref[...] + (1.0 - DECAY_RATE) * col_sum / height
    new_cols_ref[...] = new_cols
    inv_cols = 1.0 / new_cols
    col_acc[...] = jnp.broadcast_to(inv_cols, col_acc.shape)

    def square_rows(s, acc):
        at = pl.ds(pl.multiple_of(s * GROUP, GROUP), GROUP)
        row = None
        for b in range(blocks):
            lanes = slice(b * LANES, (b + 1) * LANES)
            g = gbuf[at, lanes].astype(jnp.float32)
            c = col_acc[:, lanes]
            term = g * g * jnp.concatenate([c, c], axis=0)
            row = term if row is None else row + term
        r = row_col[at, :]
        return acc + row * (r * r)

    acc = lax.fori_loop(0, rows // GROUP, square_rows, jnp.zeros((GROUP, LANES), jnp.float32))
    lane = lax.broadcasted_iota(jnp.int32, (1, LANES), 1)
    sc1_slots[mrow] = jnp.where(lane == 0, row_mass, jnp.where(lane == 1, jnp.sum(acc), 0.0))
    send_slots(sc1_slots, mrow, col_peer, s1send, s1recv, n_mrow)
    wait_slots(sc1_slots, mrow, col_peer, s1send, s1recv, n_mrow)
    sc2_slots[q] = lax.fori_loop(1, n_mrow, lambda j, a: a + sc1_slots[j], sc1_slots[0])
    send_slots(sc2_slots, q, row_peer, s2send, s2recv, n_row)
    wait_slots(sc2_slots, q, row_peer, s2send, s2recv, n_row)
    both = sc2_slots[0]
    for j in range(1, n_row):
        both = both + sc2_slots[j]
    pick = jnp.zeros((8, LANES), jnp.float32)
    total = jnp.sum(jnp.where(lane == 0, both, 0.0), axis=1, keepdims=True) / (n_row * height)
    whole = jnp.sum(jnp.where(lane == 1, both, 0.0), axis=1, keepdims=True)
    root_mean = jnp.sqrt(total * whole / (float(width) * float(height)))
    scale = jnp.sqrt(total) / jnp.maximum(1.0, root_mean / CLIP_LIMIT)
    scal_ref[0:1, :] = jnp.broadcast_to(root_mean, (1, LANES))
    scal_ref[1:2, :] = jnp.broadcast_to(scale, (1, LANES))
    col_acc[...] = jnp.broadcast_to(lax.rsqrt(new_cols) * scale, col_acc.shape)

    def weight_chunk(i):
        master_copy(i).wait()

        for k in range(1, n_dp):
            grad_copy(k, i).wait_send()

        def weight_rows(s, carry):
            at = pl.ds(pl.multiple_of(i * chunk + s * GROUP, GROUP), GROUP)
            r = row_col[at, :]
            for b in range(blocks):
                lanes = slice(b * LANES, (b + 1) * LANES)
                c = col_acc[:, lanes]
                step = gbuf[at, lanes].astype(jnp.float32) * r * jnp.concatenate([c, c], axis=0)
                recv[0, at, lanes] = (mbuf[at, lanes] - LEARN_RATE * step).astype(jnp.bfloat16)
            return carry

        lax.fori_loop(0, steps, weight_rows, 0)
        for k in range(1, n_dp):
            weight_copy(k, i).start()

    loop(0, nc, weight_chunk)

    def finish(i):
        out_copy(i).wait()
        for k in range(1, n_dp):
            weight_copy(k, i).wait()

    loop(0, nc, finish)


def final_kernel(
    n_dp, scal_ref, rows_ref, cols_ref, g_ref, master_ref, w_recv_ref,
    new_ref, weights_ref, step_ref, row_col, col_acc,
):
    chunk, wc = g_ref.shape
    dp = lax.axis_index("dp")

    @pl.when(pl.program_id(0) == 0)
    def _():
        scale = scal_ref[1:2, 0:1]
        col_acc[...] = jnp.broadcast_to(lax.rsqrt(cols_ref[...]) * scale, col_acc.shape)

    row_col[...] = jnp.broadcast_to(lax.rsqrt(rows_ref[0]), (LANES, chunk)).T

    def rows_of(start):
        def body(s, carry):
            at = pl.ds(pl.multiple_of(s * GROUP, GROUP), GROUP)
            r = row_col[at, :]
            for b in range(wc // LANES):
                lanes = slice(b * LANES, (b + 1) * LANES)
                c = col_acc[:, lanes]
                step = g_ref[at, lanes].astype(jnp.float32) * r * jnp.concatenate([c, c], axis=0)
                new = master_ref[at, lanes] - LEARN_RATE * step
                step_ref[at, lanes] = step
                new_ref[at, lanes] = new
                weights_ref[at, start + b * LANES:start + (b + 1) * LANES] = new.astype(jnp.bfloat16)
            return carry

        lax.fori_loop(0, chunk // GROUP, body, 0)

    for p in range(n_dp):
        @pl.when(dp == p)
        def _():
            rows_of(p * wc)
            for k in range(1, n_dp):
                start = (p + k) % n_dp * wc
                weights_ref[:, start:start + wc] = w_recv_ref[k - 1]


def on_device(n_dp, n_mrow, n_mcol, grad_parts, master, row_factor, col_factor):
    rows, wc = master.shape
    chunk = chunk_of(rows)
    nc = rows // chunk
    n_row = n_dp * n_mcol
    f32, bf16 = jnp.float32, jnp.bfloat16
    dma = pltpu.SemaphoreType.DMA
    anywhere = pl.BlockSpec(memory_space=pl.ANY)
    vmem = pl.BlockSpec(memory_space=pltpu.VMEM)
    peers = max(n_dp - 1, 1)
    g, w_recv, new_rows, new_cols, scal = pl.pallas_call(
        functools.partial(stats_kernel, n_dp, n_mrow, n_mcol, chunk),
        out_shape=(
            jax.ShapeDtypeStruct((rows, wc), bf16),
            jax.ShapeDtypeStruct((peers, rows, wc), bf16),
            jax.ShapeDtypeStruct((1, rows), f32),
            jax.ShapeDtypeStruct((1, wc), f32),
            jax.ShapeDtypeStruct((8, LANES), f32),
        ),
        in_specs=[anywhere, anywhere, vmem, vmem],
        out_specs=(anywhere, anywhere, vmem, vmem, vmem),
        scratch_shapes=[
            pltpu.VMEM((rows, wc), bf16),
            pltpu.VMEM((peers, rows, wc), bf16),
            pltpu.VMEM((rows, wc), f32),
            pltpu.VMEM((rows, LANES), f32),
            pltpu.VMEM((n_row, 1, rows), f32),
            pltpu.VMEM((n_mrow, 1, wc), f32),
            pltpu.VMEM((n_mrow, 1, LANES), f32),
            pltpu.VMEM((n_row, 1, LANES), f32),
            pltpu.VMEM((1, rows), f32),
            pltpu.VMEM((8, wc), f32),
            dma((nc,)), dma((peers, nc)), dma((peers, nc)),
            dma((n_row,)), dma((n_row,)), dma((n_mrow,)), dma((n_mrow,)),
            dma((n_mrow,)), dma((n_mrow,)), dma((n_row,)), dma((n_row,)),
            dma((peers, nc)), dma((peers, nc)), dma((nc,)), dma((nc,)),
        ],
        compiler_params=pltpu.CompilerParams(
            collective_id=0, has_side_effects=True, vmem_limit_bytes=56 * 2**20
        ),
        name="stats",
    )(grad_parts, master, row_factor.reshape(1, rows), col_factor.reshape(1, wc))

    tile = pl.BlockSpec((chunk, wc), lambda i: (i, 0))
    new_master, weights, step = pl.pallas_call(
        functools.partial(final_kernel, n_dp),
        grid=(nc,),
        out_shape=(
            jax.ShapeDtypeStruct((rows, wc), f32),
            jax.ShapeDtypeStruct((rows, n_dp * wc), bf16),
            jax.ShapeDtypeStruct((rows, wc), f32),
        ),
        in_specs=[
            pl.BlockSpec((8, LANES), lambda i: (0, 0)),
            pl.BlockSpec((1, 1, chunk), lambda i: (i, 0, 0)),
            pl.BlockSpec((1, wc), lambda i: (0, 0)),
            tile,
            tile,
            pl.BlockSpec((peers, chunk, wc), lambda i: (0, i, 0)),
        ],
        out_specs=(tile, pl.BlockSpec((chunk, n_dp * wc), lambda i: (i, 0)), tile),
        scratch_shapes=[pltpu.VMEM((chunk, LANES), f32), pltpu.VMEM((8, wc), f32)],
        compiler_params=pltpu.CompilerParams(vmem_limit_bytes=56 * 2**20),
        name="final",
    )(scal, new_rows.reshape(nc, 1, chunk), new_cols, g, master, w_recv)
    return (
        new_master,
        weights,
        new_rows.reshape(rows),
        new_cols.reshape(wc),
        step,
        scal[0, 0],
    )


def solution(mesh):
    placed = (P("dp", "mrow", "mcol"), P("mrow", ("mcol", "dp")), P("mrow"), P(("mcol", "dp")))
    sizes = (mesh.shape["dp"], mesh.shape["mrow"], mesh.shape["mcol"])
    return jax.shard_map(
        functools.partial(on_device, *sizes),
        mesh=mesh,
        in_specs=placed,
        out_specs=(
            P("mrow", ("mcol", "dp")),
            P("mrow", "mcol"),
            P("mrow"),
            P(("mcol", "dp")),
            P("mrow", ("mcol", "dp")),
            P(),
        ),
        check_vma=False,
    )
```

time: 218 us -> 91.7 us (0.42)
  Pallas kernels: 0 us -> 86.9 us
  blocking collectives: 71.9 us -> 0 us
  waiting for transfers between devices: 67.7 us -> 0 us
  other arithmetic: 44.5 us -> 0.63 us
  between operations: 16.6 us -> 0.66 us
  local copies, waits for them, and re-layouts: 16.8 us -> 3.1 us
    pallas_call x0 -> x2, Pallas kernels: none -> 86.9 us  [the longest x1 53.6 us: on_device(): pl.pallas_call(functools.partial(stats_kernel, n_dp, n_mrow, n_mcol, chun...]
    psum x3 -> x0, blocking collectives: 71.9 us -> none  [the longest x1 37.1 us: sum_whole(): return lax.psum(values, ('dp', 'mrow', 'mcol'))]
    all_gather x1 -> x0, waiting for transfers between devices: 35.5 us -> none  [on_device(): lax.all_gather(new_flat.astype(jnp.bfloat16), 'dp', axis=1, tiled=True)]
    reduce_scatter x1 -> x0, waiting for transfers between devices: 31.5 us -> none  [on_device(): lax.psum_scatter(grad_parts, 'dp', scatter_dimension=2, tiled=True)]
    convert_element_type x1 -> x0, other arithmetic: 27.5 us -> none  [on_device(): new_flat.astype(jnp.bfloat16)]
    reduce_sum x3 -> x0, other arithmetic: 17 us -> none  [the longest x1 8.74 us: finish(): square_total = sum_whole((jnp.sum(update * update),))[0]]
    unnamed x9 -> x5, local copies, waits for them, and re-layouts: 16.8 us -> 0.61 us
  transfers between devices with their start and end apart: 2 -> 0, of which waited for: 2 -> 0; matrix products, arithmetic and copies ran while one was open for 0% -> 0% of each run, Pallas kernels for 0% -> 0%
where the time goes in v1:
time: 91.7 us; the launch traced here: 91.3 us
  Pallas kernels  86.9 us (95%)
  local copies, waits for them, and re-layouts  3.1 us (3%)
    pallas_call x1, Pallas kernels, on_device(): pl.pallas_call(functools.partial(stats_kernel, n_dp, n_mrow, n_mcol, chun...  53.6 us
    pallas_call x1, Pallas kernels, on_device(): pl.pallas_call(functools.partial(final_kernel, n_dp), grid=(nc,), out_sha...  33.4 us

profile of v1, /device:TPU:0, one launch (start us, length us, event | category | flops | bytes accessed | tf_op | source)
XLA Modules:
  0.0 91.3 jit_solution(760711582140241667)
XLA Ops:
  0.6 1.3 %reshape.27.old_rows_ref = f32[1,2304]{1,0:T(1,128)} reshape(f32[2304]{0:T(1024)} %param.6) | data formatting | bytes 18432 | tf_op jit(solution)/shard_map/reshape | solution.py:298
  1.9 53.6 %stats.1 = (bf16[2304,2048]{1,0:T(8,128)(2,1)}, bf16[1,2304,2048]{2,1,0:T(8,128)(2,1)}, f32[1,2304]{1,0:T(1,128)}, f32[1,2048]{1,0:T(1,128)}, f32[8,128]{1,0:T(8,128)}) custom-call(bf16[1,2304,4096]{2,1,0:T(8,128)(2,1)} %grad_ref.1, f32[2304,2048]{1,0:T(8,128)} %master_ref.3, f32[1,2304]{1,0:T(1,128)} %reshape.27.old_rows_ref, f32[1,2048]{1,0:T(1,128)} %bitcast.6), custom_call_target="tpu_custom_call" | custom-call | tf_op jit(solution)/shard_map/stats/pallas_call | solution.py:267
  55.5 0.0 copy-start
  55.5 0.0 copy-start.1
  55.5 33.4 %final.1 = (f32[2304,2048]{1,0:T(8,128)}, bf16[2304,4096]{1,0:T(8,128)(2,1)}, f32[2304,2048]{1,0:T(8,128)}) custom-call(f32[8,128]{1,0:T(8,128)} %get-tuple-element.14.scal_ref, f32[9,1,256]{2,1,0:T(1,128)} %bitcast.4, f32[1,2048]{1,0:T(1,128)} %get-tuple-element.16.cols_ref, bf16[2304,2048]{1,0:T(8,128)(2,1)} %get-tuple-element.17.g_ref, ...), custom_call_target="tpu_custom_call" | custom-call | tf_op jit(solution)/shard_map/final/pallas_call | solution.py:301
  88.9 0.0 copy-done
  88.9 0.6 reduce
  89.5 1.2 %slice.3 = f32[1,1]{1,0:T(1,128)} slice(f32[8,128]{1,0:T(8,128)} %get-tuple-element.14.scal_ref), slice={[0:1], [0:1]} | slice | bytes 8 | tf_op jit(solution)/shard_map/slice | solution.py:328
  90.7 0.0 copy-done.1
  90.7 0.6 copy.11
Async XLA Ops:
  55.5 33.4 %copy-start = (f32[1,2304]{1,0:T(1,128)S(1)}, f32[1,2304]{1,0:T(1,128)}, u32[]{:S(2)}) copy-start(f32[1,2304]{1,0:T(1,128)} %get-tuple-element.15) | copy-start | bytes 27652
  55.5 35.2 %copy-start.1 = (f32[1,2048]{1,0:T(1,128)S(1)}, f32[1,2048]{1,0:T(1,128)}, u32[]{:S(2)}) copy-start(f32[1,2048]{1,0:T(1,128)} %get-tuple-element.16.cols_ref) | copy-start | bytes 24580

commit v2 on v1

--- a/solution.py
+++ b/solution.py
@@ -26,10 +26,10 @@
 def stats_kernel(
     n_dp, n_mrow, n_mcol, chunk,
     grad_ref, master_ref, old_rows_ref, old_cols_ref,
-    g_ref, w_recv_ref, new_rows_ref, new_cols_ref, scal_ref,
-    gbuf, recv, mbuf, row_col, row_slots, col_slots, sc1_slots, sc2_slots, inv_rows, col_acc,
+    gbuf, recv, w_recv_ref, mbuf, row_col, new_rows_ref, new_cols_ref, scal_ref,
+    row_slots, col_slots, sc1_slots, sc2_slots, inv_rows, col_acc,
     own_sem, gsend, grecv, rsend, rrecv, csend, crecv, s1send, s1recv, s2send, s2recv,
-    wsend, wrecv, msem, osem,
+    wsend, wrecv, msem,
 ):
     rows, wc = mbuf.shape
     nc = rows // chunk
@@ -70,9 +70,6 @@
 
     def master_copy(i):
         return pltpu.make_async_copy(master_ref.at[part(i)], mbuf.at[part(i)], msem.at[i])
-
-    def out_copy(i):
-        return pltpu.make_async_copy(gbuf.at[part(i)], g_ref.at[part(i)], osem.at[i])
 
     def weight_copy(k, i):
         return pltpu.make_async_remote_copy(
@@ -126,7 +123,6 @@
             return carry
 
         lax.fori_loop(0, steps, sum_rows, 0)
-        out_copy(i).start()
         row_slots[q, :, part(i)] = jnp.sum(row_col[part(i), :].T, axis=0, keepdims=True)
 
     loop(0, nc, sum_chunk)
@@ -176,7 +172,6 @@
     both = sc2_slots[0]
     for j in range(1, n_row):
         both = both + sc2_slots[j]
-    pick = jnp.zeros((8, LANES), jnp.float32)
     total = jnp.sum(jnp.where(lane == 0, both, 0.0), axis=1, keepdims=True) / (n_row * height)
     whole = jnp.sum(jnp.where(lane == 1, both, 0.0), axis=1, keepdims=True)
     root_mean = jnp.sqrt(total * whole / (float(width) * float(height)))
@@ -198,7 +193,9 @@
                 lanes = slice(b * LANES, (b + 1) * LANES)
                 c = col_acc[:, lanes]
                 step = gbuf[at, lanes].astype(jnp.float32) * r * jnp.concatenate([c, c], axis=0)
-                recv[0, at, lanes] = (mbuf[at, lanes] - LEARN_RATE * step).astype(jnp.bfloat16)
+                new = mbuf[at, lanes] - LEARN_RATE * step
+                mbuf[at, lanes] = new
+                recv[0, at, lanes] = new.astype(jnp.bfloat16)
             return carry
 
         lax.fori_loop(0, steps, weight_rows, 0)
@@ -208,7 +205,6 @@
     loop(0, nc, weight_chunk)
 
     def finish(i):
-        out_copy(i).wait()
         for k in range(1, n_dp):
             weight_copy(k, i).wait()
 
@@ -216,42 +212,77 @@
 
 
 def final_kernel(
-    n_dp, scal_ref, rows_ref, cols_ref, g_ref, master_ref, w_recv_ref,
-    new_ref, weights_ref, step_ref, row_col, col_acc,
+    n_dp, chunk,
+    g_ref, own_ref, w_recv_ref, master_ref, row_col, rows_ref, cols_ref, scal_ref,
+    new_ref, weights_ref, step_ref, new_rows_ref, new_cols_ref, root_ref,
+    sbuf, col_acc, nsem, wsem, rsem, ssem,
 ):
-    chunk, wc = g_ref.shape
+    rows, wc = g_ref.shape
+    nc = rows // chunk
+    slots = sbuf.shape[0]
     dp = lax.axis_index("dp")
 
-    @pl.when(pl.program_id(0) == 0)
-    def _():
-        scale = scal_ref[1:2, 0:1]
-        col_acc[...] = jnp.broadcast_to(lax.rsqrt(cols_ref[...]) * scale, col_acc.shape)
-
-    row_col[...] = jnp.broadcast_to(lax.rsqrt(rows_ref[0]), (LANES, chunk)).T
-
-    def rows_of(start):
+    def loop(lo, hi, body):
+        lax.fori_loop(lo, hi, lambda i, c: (body(i), c)[1], 0)
+
+    def part(i):
+        return pl.ds(pl.multiple_of(i * chunk, chunk), chunk)
+
+    def cols_of(k):
+        return pl.ds(pl.multiple_of(lax.rem(dp + k, n_dp) * wc, LANES), wc)
+
+    def new_copy(i):
+        return pltpu.make_async_copy(master_ref.at[part(i)], new_ref.at[part(i)], nsem.at[i])
+
+    def own_copy(i):
+        return pltpu.make_async_copy(own_ref.at[0, part(i)], weights_ref.at[part(i), cols_of(0)], wsem.at[i])
+
+    def other_copy(k, i):
+        return pltpu.make_async_copy(
+            w_recv_ref.at[k - 1, part(i)], weights_ref.at[part(i), cols_of(k)], rsem.at[k - 1, i])
+
+    def step_copy(i):
+        slot = lax.rem(i, slots)
+        return pltpu.make_async_copy(sbuf.at[slot], step_ref.at[part(i)], ssem.at[slot])
+
+    def each(act):
+        def body(i):
+            act(new_copy(i))
+            act(own_copy(i))
+            for k in range(1, n_dp):
+                act(other_copy(k, i))
+        return body
+
+    loop(0, nc, each(lambda copy: copy.start()))
+    new_rows_ref[...] = rows_ref[...]
+    new_cols_ref[...] = cols_ref[...]
+    root_ref[0, 0] = jnp.max(scal_ref[0:1, :])
+    col_acc[...] = jnp.broadcast_to(lax.rsqrt(cols_ref[...]) * scal_ref[1:2, 0:1], col_acc.shape)
+
+    def step_chunk(i):
+        slot = lax.rem(i, slots)
+
+        @pl.when(i >= slots)
+        def _():
+            step_copy(i).wait()
+
         def body(s, carry):
             at = pl.ds(pl.multiple_of(s * GROUP, GROUP), GROUP)
-            r = row_col[at, :]
+            source = pl.ds(pl.multiple_of(i * chunk + s * GROUP, GROUP), GROUP)
+            r = row_col[source, :]
             for b in range(wc // LANES):
                 lanes = slice(b * LANES, (b + 1) * LANES)
                 c = col_acc[:, lanes]
-                step = g_ref[at, lanes].astype(jnp.float32) * r * jnp.concatenate([c, c], axis=0)
-                new = master_ref[at, lanes] - LEARN_RATE * step
-                step_ref[at, lanes] = step
-                new_ref[at, lanes] = new
-                weights_ref[at, start + b * LANES:start + (b + 1) * LANES] = new.astype(jnp.bfloat16)
+                sbuf[slot, at, lanes] = (
+                    g_ref[source, lanes].astype(jnp.float32) * r * jnp.concatenate([c, c], axis=0))
             return carry
 
         lax.fori_loop(0, chunk // GROUP, body, 0)
-
-    for p in range(n_dp):
-        @pl.when(dp == p)
-        def _():
-            rows_of(p * wc)
-            for k in range(1, n_dp):
-                start = (p + k) % n_dp * wc
-                weights_ref[:, start:start + wc] = w_recv_ref[k - 1]
+        step_copy(i).start()
+
+    loop(0, nc, step_chunk)
+    loop(0, nc, each(lambda copy: copy.wait()))
+    loop(max(nc - slots, 0), nc, lambda i: step_copy(i).wait())
 
 
 def on_device(n_dp, n_mrow, n_mcol, grad_parts, master, row_factor, col_factor):
@@ -264,22 +295,22 @@
     anywhere = pl.BlockSpec(memory_space=pl.ANY)
     vmem = pl.BlockSpec(memory_space=pltpu.VMEM)
     peers = max(n_dp - 1, 1)
-    g, w_recv, new_rows, new_cols, scal = pl.pallas_call(
+    slots = min(3, nc)
+    held = pl.pallas_call(
         functools.partial(stats_kernel, n_dp, n_mrow, n_mcol, chunk),
         out_shape=(
-            jax.ShapeDtypeStruct((rows, wc), bf16),
-            jax.ShapeDtypeStruct((peers, rows, wc), bf16),
-            jax.ShapeDtypeStruct((1, rows), f32),
-            jax.ShapeDtypeStruct((1, wc), f32),
-            jax.ShapeDtypeStruct((8, LANES), f32),
-        ),
-        in_specs=[anywhere, anywhere, vmem, vmem],
-        out_specs=(anywhere, anywhere, vmem, vmem, vmem),
-        scratch_shapes=[
             pltpu.VMEM((rows, wc), bf16),
+            pltpu.VMEM((peers, rows, wc), bf16),
             pltpu.VMEM((peers, rows, wc), bf16),
             pltpu.VMEM((rows, wc), f32),
             pltpu.VMEM((rows, LANES), f32),
+            pltpu.VMEM((1, rows), f32),
+            pltpu.VMEM((1, wc), f32),
+            pltpu.VMEM((8, LANES), f32),
+        ),
+        in_specs=[anywhere, anywhere, vmem, vmem],
+        out_specs=(vmem,) * 8,
+        scratch_shapes=[
             pltpu.VMEM((n_row, 1, rows), f32),
             pltpu.VMEM((n_mrow, 1, wc), f32),
             pltpu.VMEM((n_mrow, 1, LANES), f32),
@@ -289,43 +320,40 @@
             dma((nc,)), dma((peers, nc)), dma((peers, nc)),
             dma((n_row,)), dma((n_row,)), dma((n_mrow,)), dma((n_mrow,)),
             dma((n_mrow,)), dma((n_mrow,)), dma((n_row,)), dma((n_row,)),
-            dma((peers, nc)), dma((peers, nc)), dma((nc,)), dma((nc,)),
+            dma((peers, nc)), dma((peers, nc)), dma((nc,)),
         ],
         compiler_params=pltpu.CompilerParams(
-            collective_id=0, has_side_effects=True, vmem_limit_bytes=56 * 2**20
+            collective_id=0, has_side_effects=True, vmem_limit_bytes=9 * 2**20
         ),
         name="stats",
     )(grad_parts, master, row_factor.reshape(1, rows), col_factor.reshape(1, wc))
-
-    tile = pl.BlockSpec((chunk, wc), lambda i: (i, 0))
-    new_master, weights, step = pl.pallas_call(
-        functools.partial(final_kernel, n_dp),
-        grid=(nc,),
+    held = [pltpu.with_memory_space_constraint(x, pltpu.VMEM) for x in held]
+    new_master, weights, step, new_rows, new_cols, root = pl.pallas_call(
+        functools.partial(final_kernel, n_dp, chunk),
         out_shape=(
             jax.ShapeDtypeStruct((rows, wc), f32),
             jax.ShapeDtypeStruct((rows, n_dp * wc), bf16),
             jax.ShapeDtypeStruct((rows, wc), f32),
+            jax.ShapeDtypeStruct((1, rows), f32),
+            jax.ShapeDtypeStruct((1, wc), f32),
+            jax.ShapeDtypeStruct((1, 1), f32),
         ),
-        in_specs=[
-            pl.BlockSpec((8, LANES), lambda i: (0, 0)),
-            pl.BlockSpec((1, 1, chunk), lambda i: (i, 0, 0)),
-            pl.BlockSpec((1, wc), lambda i: (0, 0)),
-            tile,
-            tile,
-            pl.BlockSpec((peers, chunk, wc), lambda i: (0, i, 0)),
+        in_specs=[vmem] * 8,
+        out_specs=(anywhere, anywhere, anywhere, vmem, vmem, pl.BlockSpec(memory_space=pltpu.SMEM)),
+        scratch_shapes=[
+            pltpu.VMEM((slots, chunk, wc), f32), pltpu.VMEM((8, wc), f32),
+            dma((nc,)), dma((nc,)), dma((peers, nc)), dma((slots,)),
         ],
-        out_specs=(tile, pl.BlockSpec((chunk, n_dp * wc), lambda i: (i, 0)), tile),
-        scratch_shapes=[pltpu.VMEM((chunk, LANES), f32), pltpu.VMEM((8, wc), f32)],
-        compiler_params=pltpu.CompilerParams(vmem_limit_bytes=56 * 2**20),
+        compiler_params=pltpu.CompilerParams(vmem_limit_bytes=9 * 2**20),
         name="final",
-    )(scal, new_rows.reshape(nc, 1, chunk), new_cols, g, master, w_recv)
+    )(*held)
     return (
         new_master,
         weights,
         new_rows.reshape(rows),
         new_cols.reshape(wc),
         step,
-        scal[0, 0],
+        root.reshape(()),
     )
 
 

time: 91.7 us -> 75.2 us (0.82)
  Pallas kernels: 86.9 us -> 71.5 us
  local copies, waits for them, and re-layouts: 3.1 us -> 1.31 us
    pallas_call x1, Pallas kernels: 33.4 us -> 18.7 us  [on_device(): pl.pallas_call(functools.partial(final_kernel, n_dp, chunk), out_shape=(j...]
    slice x1 -> x0, local copies, waits for them, and re-layouts: 1.18 us -> none  [on_device(): scal[0, 0]]
where the time goes in v2:
time: 75.2 us; the launch traced here: 74.8 us
  Pallas kernels  71.5 us (95%)
  other arithmetic  1.33 us (2%)
  local copies, waits for them, and re-layouts  1.31 us (2%)
    pallas_call x1, Pallas kernels, on_device(): pl.pallas_call(functools.partial(stats_kernel, n_dp, n_mrow, n_mcol, chun...  52.8 us
    pallas_call x1, Pallas kernels, on_device(): pl.pallas_call(functools.partial(final_kernel, n_dp, chunk), out_shape=(j...  18.7 us

profile of v2, /device:TPU:0, one launch (start us, length us, event | category | flops | bytes accessed | tf_op | source)
XLA Modules:
  0.0 74.8 jit_solution(11278613472180962903)
XLA Ops:
  0.6 1.3 %reshape.27.old_rows_ref = f32[1,2304]{1,0:T(1,128)} reshape(f32[2304]{0:T(1024)} %param.6) | data formatting | bytes 18432 | tf_op jit(solution)/shard_map/reshape | solution.py:329
  1.9 52.8 %stats.1 = (bf16[2304,2048]{1,0:T(8,128)(2,1)S(1)}, bf16[1,2304,2048]{2,1,0:T(8,128)(2,1)S(1)}, bf16[1,2304,2048]{2,1,0:T(8,128)(2,1)S(1)}, f32[2304,2048]{1,0:T...) custom-call(bf16[1,2304,4096]{2,1,0:T(8,128)(2,1)} %grad_ref.1, ...), custom_call_target="tpu_custom_call" | custom-call | tf_op jit(solution)/shard_map/stats/pallas_call | solution.py:299
  54.7 18.7 %final.1 = (f32[2304,2048]{1,0:T(8,128)}, bf16[2304,4096]{1,0:T(8,128)(2,1)}, f32[2304,2048]{1,0:T(8,128)}, f32[1,2304]{1,0:T(1,128)}, f32[1,2048]{1,0:T(1,128)}, /*index=5*/f32[1,1]{1,0:T(1,128)}) custom-call(bf16[2304,2048]{1,0:T(8,128)(2,1)S(1)} %get-tuple-element.20.g_ref, bf16[1,2304,2048]{2,1,0:T(8,128)(2,1)S(1)} %get-tuple-element.21.own_ref, ...), custom_call_target="tpu_custom_call" | custom-call | tf_op jit(solution)/shard_map/final/pallas_call | solution.py:331
  73.5 1.3 %reduce = f32[2304]{0:T(1024)} reduce(f32[1,2304]{1,0:T(1,128)} %get-tuple-element.30, f32[]{:T(128)} %constant.1), dimensions={0}, to_apply=%get-tuple-element.30.reduce_sub_computation | reduce | bytes 18436 | tf_op jit(solution)/shard_map/final/pallas_call | solution.py:331
